TPU v7x, 32 devices: a whole 2x2x4 slice. The times are simulated.
32 devices in a mesh: pair: 8 (over y, x, core), occ: 4 (over z).
Axes of the slice: x: 2, y: 2, z: 4, core: 2. Of those that a mesh axis runs over, the one named last changes fastest.
Arguments:
- half_ints: bfloat16 [4, 3072, 6144], P('occ', 'pair'), may hold values from -6 to 6
- pair_coef: bfloat16 [512, 3072], P('occ'), may hold values from -0.15625 to 0.15625
- mo_virtual: bfloat16 [5632, 6144], P('pair'), may hold values from -0.078125 to 0.078125
- screen: int32 [48], replicated, may hold values 0 or 1
- slot_block: int32 [48], replicated, may hold values from 0 to 47, each once
Outputs:
- mo_block: bfloat16 [5632, 4, 512], P('pair', 'occ')
Inputs may be any that keep to these rules, and one draw needn't show every extreme that they name: `screen`: 1 where the pair block survives screening, 0 where it is dropped. `slot_block`: each logical pair block stands in exactly one storage slot; index k of pair holds slots k * 6 to k * 6 + 5.
All inputs are finite; a program needn't handle non-finite values.
Results may differ from a plain program's by a relative error of at most 0.0049.
Values may be sent and summed in bfloat16 or wider, within the bound.
A program may use at most 128 MiB of HBM per device.

v0:
```python
import functools

import jax
import jax.numpy as jnp
from jax import lax
from jax.experimental import pallas as pl
from jax.experimental.pallas import tpu as pltpu
from jax.sharding import PartitionSpec as P

MESH = pl.DeviceIdType.MESH
WIDTH = 1024
LEAD = 1
LAG = 3


def flip(index, stride):
    return index + stride * (1 - 2 * (lax.rem(lax.div(index, stride), 2)))


def flip_by(index, mask):
    for bit in range(mask.bit_length()):
        if (mask >> bit) & 1:
            index = flip(index, 1 << bit)
    return index


def kernel(
    n_pair, n_occ, block,
    half_hbm, coef_hbm, virt_hbm, screen_ref, slot_ref,
    out_ref,
    coef_buf, half_buf, sel_buf, virt_buf, part, kept, gathered, twin, total, *rest,
):
    steps = n_pair.bit_length() - 2
    landed, sems = rest[:steps], rest[steps:]
    (coef_sem, half_local, half_send, half_recv, sel_send, sel_recv, virt_sem,
     rs_send, rs_recv, ag_send, ag_recv, twin_send, twin_recv) = sems
    me = lax.axis_index("pair")
    z = lax.axis_index("occ")
    core = lax.rem(me, 2)
    other = flip(me, 1)
    subs, _, width = half_buf.shape
    chunks, rows, _ = part.shape
    depth = half_hbm.shape[0]
    half_n = subs * width

    up = [2 << s for s in range(steps)]
    down = up[steps // 2:] + up[:steps // 2]
    stride = [a + core * (b - a) for a, b in zip(up, down)]
    partner = [flip(me, s) for s in stride]
    keep, send = [], []
    r0, c0, r, c = 0, 0, rows, width
    for s in range(steps):
        bit = lax.rem(lax.div(me, stride[s]), 2)
        if r >= 32:
            r = r // 2
            kr, kc, sr, sc = r0 + bit * r, c0, r0 + (1 - bit) * r, c0
        else:
            c = c // 2
            kr, kc, sr, sc = r0, c0 + bit * c, r0, c0 + (1 - bit) * c
        region = lambda a, b, r=r, c=c: (
            pl.ds(a if isinstance(a, int) else pl.multiple_of(a, 16), r),
            pl.ds(b if isinstance(b, int) else pl.multiple_of(b, 128), c),
        )
        keep.append(region(kr, kc))
        send.append(region(sr, sc))
        r0, c0 = kr, kc

    def half_copy(k):
        own = half_hbm.at[:, pl.ds(pl.multiple_of(core * half_n + k * width, 128), width)]
        dst = half_buf.at[k, pl.ds(pl.multiple_of(core * depth, 16), depth), :]
        return pltpu.make_async_copy(own, dst, half_local.at[k])

    def half_remote(k):
        src = half_hbm.at[:, pl.ds(pl.multiple_of((1 - core) * half_n + k * width, 128), width)]
        dst = half_buf.at[k, pl.ds(pl.multiple_of(core * depth, 16), depth), :]
        return pltpu.make_async_remote_copy(
            src, dst, half_send.at[k], half_recv.at[k], device_id={"pair": other}, device_id_type=MESH)

    def sel_remote(d):
        return pltpu.make_async_remote_copy(
            sel_buf.at[0], sel_buf.at[d], sel_send.at[d], sel_recv.at[d],
            device_id={"occ": flip_by(z, d)}, device_id_type=MESH)

    def sel_wait(d):
        return pltpu.make_async_remote_copy(
            sel_buf.at[0], sel_buf.at[d], sel_send.at[d], sel_recv.at[d],
            device_id={"occ": flip(z, 1)}, device_id_type=MESH)

    def rs_remote(s, t):
        return pltpu.make_async_remote_copy(
            part.at[(t, *send[s])], landed[s].at[t], rs_send.at[s, t], rs_recv.at[s, t],
            device_id={"pair": partner[s]}, device_id_type=MESH)

    def ag_remote(s, t):
        return pltpu.make_async_remote_copy(
            gathered.at[(t, *keep[s])], gathered.at[(t, *keep[s])], ag_send.at[s, t], ag_recv.at[s, t],
            device_id={"pair": partner[s]}, device_id_type=MESH)

    def ag_arrival(s, t):
        return pltpu.make_async_remote_copy(
            gathered.at[(t, *send[s])], gathered.at[(t, *send[s])], ag_send.at[s, t], ag_recv.at[s, t],
            device_id={"pair": partner[s]}, device_id_type=MESH)

    def twin_remote(t):
        return pltpu.make_async_remote_copy(
            gathered.at[t], twin.at[t], twin_send.at[t], twin_recv.at[t],
            device_id={"pair": other}, device_id_type=MESH)

    def coef_copy(k):
        src = coef_hbm.at[:, pl.ds(pl.multiple_of(k * 128, 128), 128)]
        return pltpu.make_async_copy(src, coef_buf.at[k], coef_sem.at[k])

    virt_copy = pltpu.make_async_copy(virt_hbm, virt_buf, virt_sem)

    barrier = pltpu.get_barrier_semaphore()
    pl.semaphore_signal(barrier, inc=1, device_id={"pair": other}, device_id_type=MESH)
    for s in range(steps):
        pl.semaphore_signal(barrier, inc=1, device_id={"pair": partner[s]}, device_id_type=MESH)
    for d in range(1, n_occ):
        pl.semaphore_signal(barrier, inc=1, device_id={"occ": flip_by(z, d)}, device_id_type=MESH)

    tiles = coef_buf.shape[0]

    def fetch(k, _):
        coef_copy(k).start()
        return 0

    def arrive(k, _):
        coef_copy(k).wait()
        return 0

    lax.fori_loop(0, tiles, fetch, 0)
    for k in range(subs):
        half_copy(k).start()
    total[...] = jnp.zeros_like(total)
    lax.fori_loop(0, tiles, arrive, 0)

    pl.semaphore_wait(barrier, steps + n_occ)
    for k in range(subs):
        half_remote(k).start()

    per = 128 // block
    slots = 2 * depth // block
    chip = lax.div(me, 2)
    lane = lax.broadcasted_iota(jnp.int32, (rows, 128), 1)
    for pos in range(slots // per):
        tile = jnp.zeros((rows, 128), jnp.float32)
        for spot in range(per):
            name = slot_ref[chip * slots + pos * per + spot]
            keepit = screen_ref[name].astype(jnp.float32)
            at = lax.rem(name, per)
            got = coef_buf[lax.div(name, per)].astype(jnp.float32) * keepit
            for shift in range(per):
                moved = pltpu.roll(got, shift * block, 1) if shift else got
                here = (lax.rem(at + shift, per) == spot).astype(jnp.float32)
                tile = tile + jnp.where(lax.div(lane, block) == spot, moved, 0.0) * here
        sel_buf[0, :, pos * 128:(pos + 1) * 128] = tile.astype(jnp.bfloat16)

    for d in range(1, n_occ):
        sel_remote(d).start()
    virt_copy.start()

    def produce(t):
        d, k = lax.div(t, subs), lax.rem(t, subs)

        @pl.when(d == 0)
        def _():
            half_copy(k).wait()
            half_remote(k).wait_recv()

        @pl.when((d > 0) & (k == 0))
        def _():
            sel_wait(d).wait_recv()

        p = jnp.dot(sel_buf[d], half_buf[k], preferred_element_type=jnp.float32)
        kept[t] = p
        part[t] = p.astype(jnp.bfloat16)
        rs_remote(0, t).start()

    def reduce(s, t):
        rs_remote(s, t).wait_recv()
        v = kept[(t, *keep[s])] + landed[s][t].astype(jnp.float32)
        if s + 1 < steps:
            kept[(t, *keep[s])] = v
            part[(t, *keep[s])] = v.astype(jnp.bfloat16)
            rs_remote(s + 1, t).start()
        else:
            gathered[(t, *keep[s])] = v.astype(jnp.bfloat16)
            ag_remote(s, t).start()

    def fold(t, buf, side):
        d, k = lax.div(t, subs), lax.rem(t, subs)
        cols = pl.ds(pl.multiple_of(side * half_n + k * width, 128), width)
        total[d] += lax.dot_general(
            virt_buf[:, cols], buf[t], (((1,), (1,)), ((), ())), preferred_element_type=jnp.float32)

    def gather(s, t):
        ag_arrival(s, t).wait_recv()
        if s > 0:
            ag_remote(s - 1, t).start()
        else:
            twin_remote(t).start()
            fold(t, gathered, core)

    def finish(t):
        twin_remote(t).wait_recv()
        fold(t, twin, 1 - core)

    stages = [functools.partial(reduce, s) for s in range(steps)]
    stages += [functools.partial(gather, s) for s in reversed(range(steps))]
    stages += [finish]

    def body(t, _):
        @pl.when(t < chunks)
        def _():
            produce(t)

        @pl.when(t == LEAD)
        def _():
            virt_copy.wait()

        for i, stage in enumerate(stages):
            u = t - LEAD - i * LAG

            @pl.when((u >= 0) & (u < chunks))
            def _():
                stage(u)
        return 0

    lax.fori_loop(0, chunks + LEAD + LAG * (len(stages) - 1), body, 0)

    for d in range(n_occ):
        if len(out_ref.shape) == 2:
            cols = pl.ds(pl.multiple_of(flip_by(z, d) * rows, 128), rows)
            out_ref[:, cols] = total[d].astype(jnp.bfloat16)
        else:
            out_ref[flip_by(z, d)] = total[d].astype(jnp.bfloat16)

    for k in range(subs):
        half_remote(k).wait_send()
    for d in range(1, n_occ):
        sel_wait(d).wait_send()

    def drain(t, _):
        for s in range(steps):
            rs_remote(s, t).wait_send()
            ag_remote(s, t).wait_send()
        twin_remote(t).wait_send()
        return 0

    lax.fori_loop(0, chunks, drain, 0)


def shards(n_pair, n_occ, half_ints, pair_coef, mo_virtual, screen, slot_block):
    rows = pair_coef.shape[0]
    basis = half_ints.shape[2]
    depth = half_ints.shape[1]
    half_ints = half_ints.reshape(depth, basis)
    block = pair_coef.shape[1] // screen.shape[0]
    width = min(WIDTH, basis // 2)
    subs = basis // 2 // width
    chunks = subs * n_occ
    virt = mo_virtual.shape[0]
    steps = n_pair.bit_length() - 2
    tiles = pair_coef.shape[1] // 128
    wide = rows % 128 == 0
    landed = []
    r, c = rows, width
    for _ in range(steps):
        r, c = (r // 2, c) if r >= 32 else (r, c // 2)
        landed.append(pltpu.VMEM((chunks, r, c), jnp.bfloat16))
    dma = pltpu.SemaphoreType.DMA
    out = pl.pallas_call(
        functools.partial(kernel, n_pair, n_occ, block),
        out_shape=jax.ShapeDtypeStruct(
            (virt, n_occ * rows) if wide else (n_occ, virt, rows), jnp.bfloat16),
        in_specs=[
            pl.BlockSpec(memory_space=pl.ANY),
            pl.BlockSpec(memory_space=pl.ANY),
            pl.BlockSpec(memory_space=pl.ANY),
            pl.BlockSpec(memory_space=pltpu.SMEM),
            pl.BlockSpec(memory_space=pltpu.SMEM),
        ],
        out_specs=pl.BlockSpec(memory_space=pltpu.VMEM),
        scratch_shapes=[
            pltpu.VMEM((tiles, rows, 128), jnp.bfloat16),
            pltpu.VMEM((subs, 2 * depth, width), jnp.bfloat16),
            pltpu.VMEM((n_occ, rows, 2 * depth), jnp.bfloat16),
            pltpu.VMEM((virt, basis), jnp.bfloat16),
            pltpu.VMEM((chunks, rows, width), jnp.bfloat16),
            pltpu.VMEM((chunks, rows, width), jnp.float32),
            pltpu.VMEM((chunks, rows, width), jnp.bfloat16),
            pltpu.VMEM((chunks, rows, width), jnp.bfloat16),
            pltpu.VMEM((n_occ, virt, rows), jnp.float32),
            *landed,
            dma((tiles,)), dma((subs,)), dma((subs,)), dma((subs,)),
            dma((n_occ,)), dma((n_occ,)), dma,
            dma((steps, chunks)), dma((steps, chunks)),
            dma((steps, chunks)), dma((steps, chunks)),
            dma((chunks,)), dma((chunks,)),
        ],
        compiler_params=pltpu.CompilerParams(
            collective_id=0, has_side_effects=True, vmem_limit_bytes=56 * 2**20),
    )(half_ints, pair_coef, mo_virtual, screen, slot_block)
    if not wide:
        out = jnp.transpose(out, (1, 0, 2))
    return out.reshape(virt, 1, n_occ * rows)


def solution(mesh):
    placed = (P("occ", "pair", None), P("occ", None), P("pair", None), P(), P())
    return jax.shard_map(
        functools.partial(shards, mesh.shape["pair"], mesh.shape["occ"]),
        mesh=mesh, in_specs=placed, out_specs=P("pair", "occ", None), check_vma=False,
    )
```

profile of v0, /device:TPU:0, one launch (start us, length us, event | category | flops | bytes accessed | tf_op | source)
XLA Modules:
  0.0 71.2 jit_solution(18003695401402275257)
XLA Ops:
  0.0 69.2 %shard_map.55 = bf16[704,512]{1,0:T(8,128)(2,1)} custom-call(bf16[384,6144]{1,0:T(8,128)(2,1)} %bitcast.2, bf16[128,3072]{1,0:T(8,128)(2,1)} %coef_hbm.1, bf16[704,6144]{1,0:T(8,128)(2,1)} %virt_hbm.1, s32[48]{0:T(128)} %screen_ref.1, s32[48]{0:T(128)} %slot_ref.1), custom_call_target="tpu_custom_call" | custom-call | tf_op jit(solution)/shard_map/pallas_call | solution.py:273
  69.2 2.0 %copy.7 = bf16[704,1,512]{2,0,1:T(8,128)(2,1)} copy(bf16[704,1,512]{2,0,1:T(8,128)(2,1)} %bitcast.3) | data formatting | bytes 1441792
where the time goes:
time: 71.4 us; the launch traced here: 71.2 us
  Pallas kernels  69.2 us (97%)
  local copies, waits for them, and re-layouts  2.01 us (3%)
    pallas_call x1, Pallas kernels, shards(): pl.pallas_call(functools.partial(kernel, n_pair, n_occ, block), out_shape...  69.2 us
    unnamed x1, local copies, waits for them, and re-layouts  2.01 us

commit v1 on v0

--- a/solution.py
+++ b/solution.py
@@ -9,8 +9,10 @@
 
 MESH = pl.DeviceIdType.MESH
 WIDTH = 1024
-LEAD = 1
-LAG = 3
+VMEM = 56 * 2**20
+REDUCE = 2, 4
+GATHER = 3, 4
+FINISH = 1
 
 
 def flip(index, stride):
@@ -24,16 +26,24 @@
     return index
 
 
+def xor(a, b, bits):
+    total = 0
+    for bit in range(bits):
+        total = total + lax.rem(lax.div(a, 1 << bit) + lax.div(b, 1 << bit), 2) * (1 << bit)
+    return total
+
+
 def kernel(
     n_pair, n_occ, block,
-    half_hbm, coef_hbm, virt_hbm, screen_ref, slot_ref,
+    half_hbm, coef_hbm, virt_hbm, screen_hbm, slot_hbm,
     out_ref,
-    coef_buf, half_buf, sel_buf, virt_buf, part, kept, gathered, twin, total, *rest,
+    coef_buf, half_buf, sel_buf, virt_buf, part, kept, gathered, twin, total,
+    screen_ref, slot_ref, *rest,
 ):
     steps = n_pair.bit_length() - 2
     landed, sems = rest[:steps], rest[steps:]
-    (coef_sem, half_local, half_send, half_recv, sel_send, sel_recv, virt_sem,
-     rs_send, rs_recv, ag_send, ag_recv, twin_send, twin_recv) = sems
+    (name_sem, coef_sem, half_local, half_send, half_recv, sel_send, sel_recv, pass_send, pass_recv,
+     virt_sem, rs_send, rs_recv, ag_send, ag_recv, twin_send, twin_recv) = sems
     me = lax.axis_index("pair")
     z = lax.axis_index("occ")
     core = lax.rem(me, 2)
@@ -68,47 +78,60 @@
     def half_copy(k):
         own = half_hbm.at[:, pl.ds(pl.multiple_of(core * half_n + k * width, 128), width)]
         dst = half_buf.at[k, pl.ds(pl.multiple_of(core * depth, 16), depth), :]
-        return pltpu.make_async_copy(own, dst, half_local.at[k])
+        return pltpu.make_async_copy(own, dst, half_local)
 
     def half_remote(k):
         src = half_hbm.at[:, pl.ds(pl.multiple_of((1 - core) * half_n + k * width, 128), width)]
         dst = half_buf.at[k, pl.ds(pl.multiple_of(core * depth, 16), depth), :]
         return pltpu.make_async_remote_copy(
-            src, dst, half_send.at[k], half_recv.at[k], device_id={"pair": other}, device_id_type=MESH)
-
-    def sel_remote(d):
-        return pltpu.make_async_remote_copy(
-            sel_buf.at[0], sel_buf.at[d], sel_send.at[d], sel_recv.at[d],
-            device_id={"occ": flip_by(z, d)}, device_id_type=MESH)
-
-    def sel_wait(d):
-        return pltpu.make_async_remote_copy(
-            sel_buf.at[0], sel_buf.at[d], sel_send.at[d], sel_recv.at[d],
-            device_id={"occ": flip(z, 1)}, device_id_type=MESH)
+            src, dst, half_send, half_recv.at[k], device_id={"pair": other}, device_id_type=MESH)
+
+    mine = pl.ds(pl.multiple_of(core * (rows // 2), 16), rows // 2)
+
+    def sel_remote(hop, way):
+        origin = sel_buf.at[z - way * hop, mine]
+        return pltpu.make_async_remote_copy(
+            origin, origin, sel_send.at[hop, (way + 1) // 2], sel_recv.at[z - way * hop],
+            device_id={"occ": z + way}, device_id_type=MESH)
+
+    def sel_pass(hop, way):
+        origin = sel_buf.at[z - way * hop, mine]
+        return pltpu.make_async_remote_copy(
+            origin, origin, pass_send.at[hop, (way + 1) // 2], pass_recv.at[z - way * hop],
+            device_id={"pair": other}, device_id_type=MESH)
+
+    def sel_arrival(sem, origin, half):
+        block = sel_buf.at[origin, half]
+        return pltpu.make_async_remote_copy(
+            block, block, sel_send.at[0, 0], sem.at[origin],
+            device_id={"pair": other}, device_id_type=MESH)
+
+    def inside(place):
+        return (place >= 0) & (place < n_occ)
 
     def rs_remote(s, t):
         return pltpu.make_async_remote_copy(
-            part.at[(t, *send[s])], landed[s].at[t], rs_send.at[s, t], rs_recv.at[s, t],
+            part.at[(t, *send[s])], landed[s].at[t], rs_send.at[s], rs_recv.at[s, t],
             device_id={"pair": partner[s]}, device_id_type=MESH)
 
     def ag_remote(s, t):
         return pltpu.make_async_remote_copy(
-            gathered.at[(t, *keep[s])], gathered.at[(t, *keep[s])], ag_send.at[s, t], ag_recv.at[s, t],
+            gathered.at[(t, *keep[s])], gathered.at[(t, *keep[s])], ag_send.at[s], ag_recv.at[s, t],
             device_id={"pair": partner[s]}, device_id_type=MESH)
 
     def ag_arrival(s, t):
         return pltpu.make_async_remote_copy(
-            gathered.at[(t, *send[s])], gathered.at[(t, *send[s])], ag_send.at[s, t], ag_recv.at[s, t],
+            gathered.at[(t, *send[s])], gathered.at[(t, *send[s])], ag_send.at[s], ag_recv.at[s, t],
             device_id={"pair": partner[s]}, device_id_type=MESH)
 
     def twin_remote(t):
         return pltpu.make_async_remote_copy(
-            gathered.at[t], twin.at[t], twin_send.at[t], twin_recv.at[t],
+            gathered.at[t], twin.at[t], twin_send, twin_recv.at[t],
             device_id={"pair": other}, device_id_type=MESH)
 
     def coef_copy(k):
         src = coef_hbm.at[:, pl.ds(pl.multiple_of(k * 128, 128), 128)]
-        return pltpu.make_async_copy(src, coef_buf.at[k], coef_sem.at[k])
+        return pltpu.make_async_copy(src, coef_buf.at[k], coef_sem)
 
     virt_copy = pltpu.make_async_copy(virt_hbm, virt_buf, virt_sem)
 
@@ -116,28 +139,30 @@
     pl.semaphore_signal(barrier, inc=1, device_id={"pair": other}, device_id_type=MESH)
     for s in range(steps):
         pl.semaphore_signal(barrier, inc=1, device_id={"pair": partner[s]}, device_id_type=MESH)
-    for d in range(1, n_occ):
-        pl.semaphore_signal(barrier, inc=1, device_id={"occ": flip_by(z, d)}, device_id_type=MESH)
+    for way in (-1, 1):
+        @pl.when(inside(z + way))
+        def _():
+            pl.semaphore_signal(barrier, inc=1, device_id={"occ": z + way}, device_id_type=MESH)
 
     tiles = coef_buf.shape[0]
+    names = [
+        pltpu.make_async_copy(screen_hbm, screen_ref, name_sem.at[0]),
+        pltpu.make_async_copy(slot_hbm, slot_ref, name_sem.at[1]),
+    ]
+    for copy in names:
+        copy.start()
 
     def fetch(k, _):
         coef_copy(k).start()
-        return 0
-
-    def arrive(k, _):
-        coef_copy(k).wait()
         return 0
 
     lax.fori_loop(0, tiles, fetch, 0)
     for k in range(subs):
         half_copy(k).start()
     total[...] = jnp.zeros_like(total)
-    lax.fori_loop(0, tiles, arrive, 0)
-
-    pl.semaphore_wait(barrier, steps + n_occ)
-    for k in range(subs):
-        half_remote(k).start()
+    for copy in names:
+        copy.wait()
+    pltpu.make_async_copy(coef_buf, coef_buf, coef_sem).wait()
 
     per = 128 // block
     slots = 2 * depth // block
@@ -154,25 +179,50 @@
                 moved = pltpu.roll(got, shift * block, 1) if shift else got
                 here = (lax.rem(at + shift, per) == spot).astype(jnp.float32)
                 tile = tile + jnp.where(lax.div(lane, block) == spot, moved, 0.0) * here
-        sel_buf[0, :, pos * 128:(pos + 1) * 128] = tile.astype(jnp.bfloat16)
-
-    for d in range(1, n_occ):
-        sel_remote(d).start()
-    virt_copy.start()
+        sel_buf[z, :, pos * 128:(pos + 1) * 128] = tile.astype(jnp.bfloat16)
+
+    pl.semaphore_wait(barrier, 1 + steps + inside(z - 1).astype(jnp.int32) + inside(z + 1).astype(jnp.int32))
+    for k in range(subs):
+        half_remote(k).start()
+    for way in (-1, 1):
+        @pl.when(inside(z + way))
+        def _():
+            sel_remote(0, way).start()
+
+    def relay(hop):
+        for way in (-1, 1):
+            origin = z - way * hop
+
+            @pl.when(inside(origin))
+            def _():
+                sel_arrival(sel_recv, origin, mine).wait_recv()
+
+                @pl.when(inside(z + way))
+                def _():
+                    sel_remote(hop, way).start()
+
+                sel_pass(hop, way).start()
 
     def produce(t):
         d, k = lax.div(t, subs), lax.rem(t, subs)
 
+        origin = xor(z, d, (n_occ - 1).bit_length())
+
+        @pl.when(t == 0)
+        def _():
+            for k in range(subs):
+                half_copy(k).wait()
+
         @pl.when(d == 0)
         def _():
-            half_copy(k).wait()
             half_remote(k).wait_recv()
 
         @pl.when((d > 0) & (k == 0))
         def _():
-            sel_wait(d).wait_recv()
-
-        p = jnp.dot(sel_buf[d], half_buf[k], preferred_element_type=jnp.float32)
+            theirs = pl.ds(pl.multiple_of((1 - core) * (rows // 2), 16), rows // 2)
+            sel_arrival(pass_recv, origin, theirs).wait_recv()
+
+        p = jnp.dot(sel_buf[origin], half_buf[k], preferred_element_type=jnp.float32)
         kept[t] = p
         part[t] = p.astype(jnp.bfloat16)
         rs_remote(0, t).start()
@@ -205,50 +255,72 @@
     def finish(t):
         twin_remote(t).wait_recv()
         fold(t, twin, 1 - core)
+        d, k = lax.div(t, subs), lax.rem(t, subs)
+        origin = xor(z, d, (n_occ - 1).bit_length())
+
+        @pl.when(k == subs - 1)
+        def _():
+            if len(out_ref.shape) == 2:
+                cols = pl.ds(pl.multiple_of(origin * rows, 128), rows)
+                out_ref[:, cols] = total[d].astype(jnp.bfloat16)
+            else:
+                out_ref[origin] = total[d].astype(jnp.bfloat16)
 
     stages = [functools.partial(reduce, s) for s in range(steps)]
     stages += [functools.partial(gather, s) for s in reversed(range(steps))]
     stages += [finish]
+    gaps = [REDUCE[min(s, 1)] for s in range(steps)]
+    gaps += [GATHER[0]] + [GATHER[1]] * (steps - 1) + [FINISH]
+    delay = [sum(gaps[:i + 1]) for i in range(len(gaps))]
 
     def body(t, _):
         @pl.when(t < chunks)
         def _():
             produce(t)
 
-        @pl.when(t == LEAD)
+        @pl.when(t == subs)
+        def _():
+            virt_copy.start()
+
+        @pl.when(t == delay[-2])
         def _():
             virt_copy.wait()
 
-        for i, stage in enumerate(stages):
-            u = t - LEAD - i * LAG
+        for stage, late in zip(stages, delay):
+            u = t - late
 
             @pl.when((u >= 0) & (u < chunks))
             def _():
                 stage(u)
+
+        for hop in range(1, n_occ):
+            @pl.when(t == hop * subs - 1)
+            def _():
+                relay(hop)
         return 0
 
-    lax.fori_loop(0, chunks + LEAD + LAG * (len(stages) - 1), body, 0)
-
-    for d in range(n_occ):
-        if len(out_ref.shape) == 2:
-            cols = pl.ds(pl.multiple_of(flip_by(z, d) * rows, 128), rows)
-            out_ref[:, cols] = total[d].astype(jnp.bfloat16)
-        else:
-            out_ref[flip_by(z, d)] = total[d].astype(jnp.bfloat16)
-
-    for k in range(subs):
-        half_remote(k).wait_send()
-    for d in range(1, n_occ):
-        sel_wait(d).wait_send()
-
-    def drain(t, _):
-        for s in range(steps):
-            rs_remote(s, t).wait_send()
-            ag_remote(s, t).wait_send()
-        twin_remote(t).wait_send()
-        return 0
-
-    lax.fori_loop(0, chunks, drain, 0)
+    lax.fori_loop(0, chunks + delay[-1], body, 0)
+
+    half_all = half_hbm.at[:, pl.ds(0, half_n)]
+    pltpu.make_async_remote_copy(
+        half_all, half_all, half_send, half_recv.at[0], device_id={"pair": other}, device_id_type=MESH).wait_send()
+    for hop in range(n_occ):
+        for way in (-1, 1):
+            @pl.when(inside(z - way * hop) & inside(z + way))
+            def _():
+                sel_remote(hop, way).wait_send()
+
+            if hop:
+                @pl.when(inside(z - way * hop))
+                def _():
+                    sel_pass(hop, way).wait_send()
+    for s in range(steps):
+        for sem in (rs_send, ag_send):
+            pltpu.make_async_remote_copy(
+                landed[s], landed[s], sem.at[s], rs_recv.at[s, 0],
+                device_id={"pair": partner[s]}, device_id_type=MESH).wait_send()
+    pltpu.make_async_remote_copy(
+        gathered, twin, twin_send, twin_recv.at[0], device_id={"pair": other}, device_id_type=MESH).wait_send()
 
 
 def shards(n_pair, n_occ, half_ints, pair_coef, mo_virtual, screen, slot_block):
@@ -272,15 +344,9 @@
     dma = pltpu.SemaphoreType.DMA
     out = pl.pallas_call(
         functools.partial(kernel, n_pair, n_occ, block),
-        out_shape=jax.ShapeDtypeStruct(
+        out_shape=pltpu.VMEM(
             (virt, n_occ * rows) if wide else (n_occ, virt, rows), jnp.bfloat16),
-        in_specs=[
-            pl.BlockSpec(memory_space=pl.ANY),
-            pl.BlockSpec(memory_space=pl.ANY),
-            pl.BlockSpec(memory_space=pl.ANY),
-            pl.BlockSpec(memory_space=pltpu.SMEM),
-            pl.BlockSpec(memory_space=pltpu.SMEM),
-        ],
+        in_specs=[pl.BlockSpec(memory_space=pltpu.HBM)] * 5,
         out_specs=pl.BlockSpec(memory_space=pltpu.VMEM),
         scratch_shapes=[
             pltpu.VMEM((tiles, rows, 128), jnp.bfloat16),
@@ -292,15 +358,16 @@
             pltpu.VMEM((chunks, rows, width), jnp.bfloat16),
             pltpu.VMEM((chunks, rows, width), jnp.bfloat16),
             pltpu.VMEM((n_occ, virt, rows), jnp.float32),
+            pltpu.SMEM(screen.shape, jnp.int32),
+            pltpu.SMEM(slot_block.shape, jnp.int32),
             *landed,
-            dma((tiles,)), dma((subs,)), dma((subs,)), dma((subs,)),
-            dma((n_occ,)), dma((n_occ,)), dma,
-            dma((steps, chunks)), dma((steps, chunks)),
-            dma((steps, chunks)), dma((steps, chunks)),
-            dma((chunks,)), dma((chunks,)),
+            dma((2,)), dma, dma, dma, dma((subs,)),
+            dma((n_occ, 2)), dma((n_occ,)), dma((n_occ, 2)), dma((n_occ,)), dma,
+            dma((steps,)), dma((steps, chunks)), dma((steps,)), dma((steps, chunks)),
+            dma, dma((chunks,)),
         ],
         compiler_params=pltpu.CompilerParams(
-            collective_id=0, has_side_effects=True, vmem_limit_bytes=56 * 2**20),
+            collective_id=0, has_side_effects=True, vmem_limit_bytes=VMEM),
     )(half_ints, pair_coef, mo_virtual, screen, slot_block)
     if not wide:
         out = jnp.transpose(out, (1, 0, 2))

time: 71.4 us -> 63 us (0.88)
  Pallas kernels: 69.2 us -> 62 us
  local copies, waits for them, and re-layouts: 2.01 us -> 0.86 us
    pallas_call x1, Pallas kernels: 69.2 us -> 62 us  [shards(): pl.pallas_call(functools.partial(kernel, n_pair, n_occ, block), out_shape...]
    unnamed x1, local copies, waits for them, and re-layouts: 2.01 us -> 0.86 us
where the time goes in v1:
time: 63 us; the launch traced here: 62.9 us
  Pallas kernels  62 us (98%)
  local copies, waits for them, and re-layouts  0.86 us (1%)
    pallas_call x1, Pallas kernels, shards(): pl.pallas_call(functools.partial(kernel, n_pair, n_occ, block), out_shape...  62 us

profile of v1, /device:TPU:0, one launch (start us, length us, event | category | flops | bytes accessed | tf_op | source)
XLA Modules:
  0.0 62.9 jit_solution(1525924113494920976)
XLA Ops:
  0.0 62.0 %shard_map.55 = bf16[704,512]{1,0:T(8,128)(2,1)S(1)} custom-call(bf16[384,6144]{1,0:T(8,128)(2,1)} %bitcast.3, bf16[128,3072]{1,0:T(8,128)(2,1)} %coef_hbm.1, bf16[704,6144]{1,0:T(8,128)(2,1)} %virt_hbm.1, s32[48]{0:T(128)} %screen_hbm.1, s32[48]{0:T(128)} %slot_hbm.1), custom_call_target="tpu_custom_call" | custom-call | tf_op jit(solution)/shard_map/pallas_call | solution.py:345
  62.0 0.9 %copy.7 = bf16[704,1,512]{2,0,1:T(8,128)(2,1)} copy(bf16[704,1,512]{2,0,1:T(8,128)(2,1)S(1)} %bitcast.2) | data formatting | bytes 1441792

commit v2 on v1

--- a/solution.py
+++ b/solution.py
@@ -9,6 +9,7 @@
 
 MESH = pl.DeviceIdType.MESH
 WIDTH = 1024
+PIECE = 256
 VMEM = 56 * 2**20
 REDUCE = 2, 4
 GATHER = 3, 4
@@ -80,11 +81,14 @@
         dst = half_buf.at[k, pl.ds(pl.multiple_of(core * depth, 16), depth), :]
         return pltpu.make_async_copy(own, dst, half_local)
 
-    def half_remote(k):
-        src = half_hbm.at[:, pl.ds(pl.multiple_of((1 - core) * half_n + k * width, 128), width)]
-        dst = half_buf.at[k, pl.ds(pl.multiple_of(core * depth, 16), depth), :]
-        return pltpu.make_async_remote_copy(
-            src, dst, half_send, half_recv.at[k], device_id={"pair": other}, device_id_type=MESH)
+    pieces = half_recv.shape[0] // subs
+    piece = width // pieces
+
+    def half_remote(k, q):
+        src = half_hbm.at[:, pl.ds(pl.multiple_of((1 - core) * half_n + k * width + q * piece, 128), piece)]
+        dst = half_buf.at[k, pl.ds(pl.multiple_of(core * depth, 16), depth), q * piece:(q + 1) * piece]
+        return pltpu.make_async_remote_copy(
+            src, dst, half_send, half_recv.at[k * pieces + q], device_id={"pair": other}, device_id_type=MESH)
 
     mine = pl.ds(pl.multiple_of(core * (rows // 2), 16), rows // 2)
 
@@ -97,7 +101,7 @@
     def sel_pass(hop, way):
         origin = sel_buf.at[z - way * hop, mine]
         return pltpu.make_async_remote_copy(
-            origin, origin, pass_send.at[hop, (way + 1) // 2], pass_recv.at[z - way * hop],
+            origin, origin, pass_send, pass_recv.at[z - way * hop],
             device_id={"pair": other}, device_id_type=MESH)
 
     def sel_arrival(sem, origin, half):
@@ -114,6 +118,14 @@
             part.at[(t, *send[s])], landed[s].at[t], rs_send.at[s], rs_recv.at[s, t],
             device_id={"pair": partner[s]}, device_id_type=MESH)
 
+    def rs_piece(t, q):
+        if pieces == 1:
+            return rs_remote(0, t)
+        cols = slice(q * piece, (q + 1) * piece)
+        return pltpu.make_async_remote_copy(
+            part.at[t, send[0][0], cols], landed[0].at[t, :, cols], rs_send.at[0], rs_recv.at[0, t],
+            device_id={"pair": partner[0]}, device_id_type=MESH)
+
     def ag_remote(s, t):
         return pltpu.make_async_remote_copy(
             gathered.at[(t, *keep[s])], gathered.at[(t, *keep[s])], ag_send.at[s], ag_recv.at[s, t],
@@ -123,6 +135,11 @@
         return pltpu.make_async_remote_copy(
             gathered.at[(t, *send[s])], gathered.at[(t, *send[s])], ag_send.at[s], ag_recv.at[s, t],
             device_id={"pair": partner[s]}, device_id_type=MESH)
+
+    def twin_part(t, region):
+        return pltpu.make_async_remote_copy(
+            gathered.at[(t, *region)], twin.at[(t, *region)], twin_send, twin_recv.at[t],
+            device_id={"pair": other}, device_id_type=MESH)
 
     def twin_remote(t):
         return pltpu.make_async_remote_copy(
@@ -159,7 +176,12 @@
     lax.fori_loop(0, tiles, fetch, 0)
     for k in range(subs):
         half_copy(k).start()
-    total[...] = jnp.zeros_like(total)
+
+    pl.semaphore_wait(barrier, 1 + steps + inside(z - 1).astype(jnp.int32) + inside(z + 1).astype(jnp.int32))
+    for k in range(subs):
+        for q in range(pieces):
+            half_remote(k, q).start()
+
     for copy in names:
         copy.wait()
     pltpu.make_async_copy(coef_buf, coef_buf, coef_sem).wait()
@@ -181,9 +203,6 @@
                 tile = tile + jnp.where(lax.div(lane, block) == spot, moved, 0.0) * here
         sel_buf[z, :, pos * 128:(pos + 1) * 128] = tile.astype(jnp.bfloat16)
 
-    pl.semaphore_wait(barrier, 1 + steps + inside(z - 1).astype(jnp.int32) + inside(z + 1).astype(jnp.int32))
-    for k in range(subs):
-        half_remote(k).start()
     for way in (-1, 1):
         @pl.when(inside(z + way))
         def _():
@@ -213,19 +232,28 @@
             for k in range(subs):
                 half_copy(k).wait()
 
+        def make(q, part_of):
+            cols = slice(q * part_of, (q + 1) * part_of)
+            p = jnp.dot(sel_buf[origin], half_buf[k, :, cols], preferred_element_type=jnp.float32)
+            kept[t, :, cols] = p
+            part[t, :, cols] = p.astype(jnp.bfloat16)
+
         @pl.when(d == 0)
         def _():
-            half_remote(k).wait_recv()
+            for q in range(pieces):
+                half_remote(k, q).wait_recv()
+                make(q, piece)
+                rs_piece(t, q).start()
 
         @pl.when((d > 0) & (k == 0))
         def _():
             theirs = pl.ds(pl.multiple_of((1 - core) * (rows // 2), 16), rows // 2)
             sel_arrival(pass_recv, origin, theirs).wait_recv()
 
-        p = jnp.dot(sel_buf[origin], half_buf[k], preferred_element_type=jnp.float32)
-        kept[t] = p
-        part[t] = p.astype(jnp.bfloat16)
-        rs_remote(0, t).start()
+        @pl.when(d > 0)
+        def _():
+            make(0, width)
+            rs_remote(0, t).start()
 
     def reduce(s, t):
         rs_remote(s, t).wait_recv()
@@ -237,6 +265,7 @@
         else:
             gathered[(t, *keep[s])] = v.astype(jnp.bfloat16)
             ag_remote(s, t).start()
+            twin_part(t, keep[s]).start()
 
     def fold(t, buf, side):
         d, k = lax.div(t, subs), lax.rem(t, subs)
@@ -248,8 +277,8 @@
         ag_arrival(s, t).wait_recv()
         if s > 0:
             ag_remote(s - 1, t).start()
-        else:
-            twin_remote(t).start()
+        twin_part(t, send[s]).start()
+        if s == 0:
             fold(t, gathered, core)
 
     def finish(t):
@@ -281,6 +310,7 @@
         @pl.when(t == subs)
         def _():
             virt_copy.start()
+            total[...] = jnp.zeros_like(total)
 
         @pl.when(t == delay[-2])
         def _():
@@ -310,10 +340,9 @@
             def _():
                 sel_remote(hop, way).wait_send()
 
-            if hop:
-                @pl.when(inside(z - way * hop))
-                def _():
-                    sel_pass(hop, way).wait_send()
+    passed = sel_buf.at[pl.ds(0, n_occ - 1), mine]
+    pltpu.make_async_remote_copy(
+        passed, passed, pass_send, pass_recv.at[0], device_id={"pair": other}, device_id_type=MESH).wait_send()
     for s in range(steps):
         for sem in (rs_send, ag_send):
             pltpu.make_async_remote_copy(
@@ -361,8 +390,8 @@
             pltpu.SMEM(screen.shape, jnp.int32),
             pltpu.SMEM(slot_block.shape, jnp.int32),
             *landed,
-            dma((2,)), dma, dma, dma, dma((subs,)),
-            dma((n_occ, 2)), dma((n_occ,)), dma((n_occ, 2)), dma((n_occ,)), dma,
+            dma((2,)), dma, dma, dma, dma((subs * (width // PIECE if rows >= 32 and width % PIECE == 0 else 1),)),
+            dma((n_occ, 2)), dma((n_occ,)), dma, dma((n_occ,)), dma,
             dma((steps,)), dma((steps, chunks)), dma((steps,)), dma((steps, chunks)),
             dma, dma((chunks,)),
         ],

time: 63 us -> 62.1 us (0.986)
  Pallas kernels: 62 us -> 61.1 us
    pallas_call x1, Pallas kernels: 62 us -> 61.1 us  [shards(): pl.pallas_call(functools.partial(kernel, n_pair, n_occ, block), out_shape...]
where the time goes in v2:
time: 62.1 us; the launch traced here: 61.9 us
  Pallas kernels  61.1 us (98%)
  local copies, waits for them, and re-layouts  0.86 us (1%)
    pallas_call x1, Pallas kernels, shards(): pl.pallas_call(functools.partial(kernel, n_pair, n_occ, block), out_shape...  61.1 us

profile of v2, /device:TPU:0, one launch (start us, length us, event | category | flops | bytes accessed | tf_op | source)
XLA Modules:
  0.0 61.9 jit_solution(16442746069979778085)
XLA Ops:
  0.0 61.1 %shard_map.55 = bf16[704,512]{1,0:T(8,128)(2,1)S(1)} custom-call(bf16[384,6144]{1,0:T(8,128)(2,1)} %bitcast.3, bf16[128,3072]{1,0:T(8,128)(2,1)} %coef_hbm.1, bf16[704,6144]{1,0:T(8,128)(2,1)} %virt_hbm.1, s32[48]{0:T(128)} %screen_hbm.1, s32[48]{0:T(128)} %slot_hbm.1), custom_call_target="tpu_custom_call" | custom-call | tf_op jit(solution)/shard_map/pallas_call | solution.py:374
  61.1 0.9 %copy.7 = bf16[704,1,512]{2,0,1:T(8,128)(2,1)} copy(bf16[704,1,512]{2,0,1:T(8,128)(2,1)S(1)} %bitcast.2) | data formatting | bytes 1441792

commit v3 on v2

--- a/solution.py
+++ b/solution.py
@@ -10,9 +10,10 @@
 MESH = pl.DeviceIdType.MESH
 WIDTH = 1024
 PIECE = 256
+EARLY = 1
 VMEM = 56 * 2**20
-REDUCE = 2, 4
-GATHER = 3, 4
+REDUCE = 2, 3
+GATHER = 3, 3
 FINISH = 1
 
 
@@ -238,19 +239,27 @@
             kept[t, :, cols] = p
             part[t, :, cols] = p.astype(jnp.bfloat16)
 
-        @pl.when(d == 0)
+        @pl.when((d > 0) & (k == 0))
+        def _():
+            theirs = pl.ds(pl.multiple_of((1 - core) * (rows // 2), 16), rows // 2)
+            sel_arrival(pass_recv, origin, theirs).wait_recv()
+
+        @pl.when(t < subs + EARLY)
         def _():
             for q in range(pieces):
-                half_remote(k, q).wait_recv()
+                if q == pieces - 1 and n_occ > 1:
+                    @pl.when(t == subs - 1)
+                    def _():
+                        relay(1)
+
+                @pl.when(d == 0)
+                def _():
+                    half_remote(k, q).wait_recv()
+
                 make(q, piece)
                 rs_piece(t, q).start()
 
-        @pl.when((d > 0) & (k == 0))
-        def _():
-            theirs = pl.ds(pl.multiple_of((1 - core) * (rows // 2), 16), rows // 2)
-            sel_arrival(pass_recv, origin, theirs).wait_recv()
-
-        @pl.when(d > 0)
+        @pl.when(t >= subs + EARLY)
         def _():
             make(0, width)
             rs_remote(0, t).start()
@@ -323,7 +332,7 @@
             def _():
                 stage(u)
 
-        for hop in range(1, n_occ):
+        for hop in range(2, n_occ):
             @pl.when(t == hop * subs - 1)
             def _():
                 relay(hop)

time: 62.1 us -> 61.4 us (0.989)
  Pallas kernels: 61.1 us -> 60.4 us
    pallas_call x1, Pallas kernels: 61.1 us -> 60.4 us  [shards(): pl.pallas_call(functools.partial(kernel, n_pair, n_occ, block), out_shape...]
where the time goes in v3:
time: 61.4 us; the launch traced here: 61.3 us
  Pallas kernels  60.4 us (98%)
  local copies, waits for them, and re-layouts  0.86 us (1%)
    pallas_call x1, Pallas kernels, shards(): pl.pallas_call(functools.partial(kernel, n_pair, n_occ, block), out_shape...  60.4 us

profile of v3, /device:TPU:0, one launch (start us, length us, event | category | flops | bytes accessed | tf_op | source)
XLA Modules:
  0.0 61.3 jit_solution(2548815301122030571)
XLA Ops:
  0.0 60.4 %shard_map.55 = bf16[704,512]{1,0:T(8,128)(2,1)S(1)} custom-call(bf16[384,6144]{1,0:T(8,128)(2,1)} %bitcast.3, bf16[128,3072]{1,0:T(8,128)(2,1)} %coef_hbm.1, bf16[704,6144]{1,0:T(8,128)(2,1)} %virt_hbm.1, s32[48]{0:T(128)} %screen_hbm.1, s32[48]{0:T(128)} %slot_hbm.1), custom_call_target="tpu_custom_call" | custom-call | tf_op jit(solution)/shard_map/pallas_call | solution.py:383
  60.4 0.9 %copy.7 = bf16[704,1,512]{2,0,1:T(8,128)(2,1)} copy(bf16[704,1,512]{2,0,1:T(8,128)(2,1)S(1)} %bitcast.2) | data formatting | bytes 1441792

commit v4 on v2

--- a/solution.py
+++ b/solution.py
@@ -11,8 +11,8 @@
 WIDTH = 1024
 PIECE = 256
 VMEM = 56 * 2**20
-REDUCE = 2, 4
-GATHER = 3, 4
+REDUCE = 2, 3
+GATHER = 3, 3
 FINISH = 1
 
 
@@ -238,22 +238,23 @@
             kept[t, :, cols] = p
             part[t, :, cols] = p.astype(jnp.bfloat16)
 
-        @pl.when(d == 0)
-        def _():
-            for q in range(pieces):
-                half_remote(k, q).wait_recv()
-                make(q, piece)
-                rs_piece(t, q).start()
-
         @pl.when((d > 0) & (k == 0))
         def _():
             theirs = pl.ds(pl.multiple_of((1 - core) * (rows // 2), 16), rows // 2)
             sel_arrival(pass_recv, origin, theirs).wait_recv()
 
-        @pl.when(d > 0)
-        def _():
-            make(0, width)
-            rs_remote(0, t).start()
+        for q in range(pieces):
+            if q == pieces - 1 and n_occ > 1:
+                @pl.when(t == subs - 1)
+                def _():
+                    relay(1)
+
+            @pl.when(d == 0)
+            def _():
+                half_remote(k, q).wait_recv()
+
+            make(q, piece)
+            rs_piece(t, q).start()
 
     def reduce(s, t):
         rs_remote(s, t).wait_recv()
@@ -323,7 +324,7 @@
             def _():
                 stage(u)
 
-        for hop in range(1, n_occ):
+        for hop in range(2, n_occ):
             @pl.when(t == hop * subs - 1)
             def _():
                 relay(hop)

time: 62.1 us -> 61.4 us (0.989)
  Pallas kernels: 61.1 us -> 60.4 us
    pallas_call x1, Pallas kernels: 61.1 us -> 60.4 us  [shards(): pl.pallas_call(functools.partial(kernel, n_pair, n_occ, block), out_shape...]
where the time goes in v4:
time: 61.4 us; the launch traced here: 61.2 us
  Pallas kernels  60.4 us (98%)
  local copies, waits for them, and re-layouts  0.86 us (1%)
    pallas_call x1, Pallas kernels, shards(): pl.pallas_call(functools.partial(kernel, n_pair, n_occ, block), out_shape...  60.4 us

profile of v4, /device:TPU:0, one launch (start us, length us, event | category | flops | bytes accessed | tf_op | source)
XLA Modules:
  0.0 61.2 jit_solution(17481009998507849666)
XLA Ops:
  0.0 60.4 %shard_map.55 = bf16[704,512]{1,0:T(8,128)(2,1)S(1)} custom-call(bf16[384,6144]{1,0:T(8,128)(2,1)} %bitcast.3, bf16[128,3072]{1,0:T(8,128)(2,1)} %coef_hbm.1, bf16[704,6144]{1,0:T(8,128)(2,1)} %virt_hbm.1, s32[48]{0:T(128)} %screen_hbm.1, s32[48]{0:T(128)} %slot_hbm.1), custom_call_target="tpu_custom_call" | custom-call | tf_op jit(solution)/shard_map/pallas_call | solution.py:375
  60.4 0.9 %copy.7 = bf16[704,1,512]{2,0,1:T(8,128)(2,1)} copy(bf16[704,1,512]{2,0,1:T(8,128)(2,1)S(1)} %bitcast.2) | data formatting | bytes 1441792

commit v5 on v3

--- a/solution.py
+++ b/solution.py
@@ -54,6 +54,7 @@
     chunks, rows, _ = part.shape
     depth = half_hbm.shape[0]
     half_n = subs * width
+    ring = rs_recv.shape[1]
 
     up = [2 << s for s in range(steps)]
     down = up[steps // 2:] + up[:steps // 2]
@@ -116,7 +117,7 @@
 
     def rs_remote(s, t):
         return pltpu.make_async_remote_copy(
-            part.at[(t, *send[s])], landed[s].at[t], rs_send.at[s], rs_recv.at[s, t],
+            part.at[(t, *send[s])], landed[s].at[t], rs_send.at[s], rs_recv.at[s, lax.rem(t, ring)],
             device_id={"pair": partner[s]}, device_id_type=MESH)
 
     def rs_piece(t, q):
@@ -124,17 +125,17 @@
             return rs_remote(0, t)
         cols = slice(q * piece, (q + 1) * piece)
         return pltpu.make_async_remote_copy(
-            part.at[t, send[0][0], cols], landed[0].at[t, :, cols], rs_send.at[0], rs_recv.at[0, t],
+            part.at[t, send[0][0], cols], landed[0].at[t, :, cols], rs_send.at[0], rs_recv.at[0, lax.rem(t, ring)],
             device_id={"pair": partner[0]}, device_id_type=MESH)
 
     def ag_remote(s, t):
         return pltpu.make_async_remote_copy(
-            gathered.at[(t, *keep[s])], gathered.at[(t, *keep[s])], ag_send.at[s], ag_recv.at[s, t],
+            gathered.at[(t, *keep[s])], gathered.at[(t, *keep[s])], ag_send.at[s], ag_recv.at[s, lax.rem(t, ring)],
             device_id={"pair": partner[s]}, device_id_type=MESH)
 
     def ag_arrival(s, t):
         return pltpu.make_async_remote_copy(
-            gathered.at[(t, *send[s])], gathered.at[(t, *send[s])], ag_send.at[s], ag_recv.at[s, t],
+            gathered.at[(t, *send[s])], gathered.at[(t, *send[s])], ag_send.at[s], ag_recv.at[s, lax.rem(t, ring)],
             device_id={"pair": partner[s]}, device_id_type=MESH)
 
     def twin_part(t, region):
@@ -374,6 +375,7 @@
     steps = n_pair.bit_length() - 2
     tiles = pair_coef.shape[1] // 128
     wide = rows % 128 == 0
+    ring = min(chunks, 2 * (max(*REDUCE, *GATHER) + 1))
     landed = []
     r, c = rows, width
     for _ in range(steps):
@@ -401,7 +403,7 @@
             *landed,
             dma((2,)), dma, dma, dma, dma((subs * (width // PIECE if rows >= 32 and width % PIECE == 0 else 1),)),
             dma((n_occ, 2)), dma((n_occ,)), dma, dma((n_occ,)), dma,
-            dma((steps,)), dma((steps, chunks)), dma((steps,)), dma((steps, chunks)),
+            dma((steps,)), dma((steps, ring)), dma((steps,)), dma((steps, ring)),
             dma, dma((chunks,)),
         ],
         compiler_params=pltpu.CompilerParams(

time: 61.4 us -> 61.3 us (level)
  no operation moved by 1% of the time
where the time goes in v5:
time: 61.3 us; the launch traced here: 61.1 us
  Pallas kernels  60.2 us (98%)
  local copies, waits for them, and re-layouts  0.86 us (1%)
    pallas_call x1, Pallas kernels, shards(): pl.pallas_call(functools.partial(kernel, n_pair, n_occ, block), out_shape...  60.2 us

profile of v5, /device:TPU:0, one launch (start us, length us, event | category | flops | bytes accessed | tf_op | source)
XLA Modules:
  0.0 61.1 jit_solution(1205063643779034549)
XLA Ops:
  0.0 60.2 %shard_map.55 = bf16[704,512]{1,0:T(8,128)(2,1)S(1)} custom-call(bf16[384,6144]{1,0:T(8,128)(2,1)} %bitcast.3, bf16[128,3072]{1,0:T(8,128)(2,1)} %coef_hbm.1, bf16[704,6144]{1,0:T(8,128)(2,1)} %virt_hbm.1, s32[48]{0:T(128)} %screen_hbm.1, s32[48]{0:T(128)} %slot_hbm.1), custom_call_target="tpu_custom_call" | custom-call | tf_op jit(solution)/shard_map/pallas_call | solution.py:385
  60.2 0.9 %copy.7 = bf16[704,1,512]{2,0,1:T(8,128)(2,1)} copy(bf16[704,1,512]{2,0,1:T(8,128)(2,1)S(1)} %bitcast.2) | data formatting | bytes 1441792
